TPU v7x, 32 devices: a whole 2x2x4 slice. The times are simulated.
32 devices in a mesh: dp: 8 (over z, x), mp: 4 (over y, core).
Axes of the slice: x: 2, y: 2, z: 4, core: 2. Of those that a mesh axis runs over, the one named last changes fastest.
Arguments:
- tokens: bfloat16 [32768, 1024], P('dp'), may hold values from -12 to 12
- out_grad: bfloat16 [32768, 1024], P('dp'), may hold values from -12 to 12
- qk_weight: float32 [2, 1024, 256], P(None, 'dp'), may hold values from -0.1875 to 0.1875
- qk_first: float32 [2, 1024, 256], P(None, 'dp'), may hold values from -0.0048828125 to 0.0048828125
- qk_second: float32 [2, 1024, 256], P(None, 'dp'), may hold values from 5.839972e-07 to 2.3359887e-06
- qk_average: float32 [2, 1024, 256], P(None, 'dp'), may hold values from -0.1875 to 0.1875
- value_weight: float32 [1024, 1024], P('dp', 'mp'), may hold values from -0.1875 to 0.1875
- value_first: float32 [1024, 1024], P('dp', 'mp'), may hold values from -0.0024414062 to 0.0024414062
- value_second: float32 [1024, 1024], P('dp', 'mp'), may hold values from 1.9069296e-07 to 7.6277183e-07
- value_average: float32 [1024, 1024], P('dp', 'mp'), may hold values from -0.1875 to 0.1875
- output_weight: float32 [1024, 1024], P('mp', 'dp'), may hold values from -1.5 to 1.5
- output_first: float32 [1024, 1024], P('mp', 'dp'), may hold values from -0.00048828125 to 0.00048828125
- output_second: float32 [1024, 1024], P('mp', 'dp'), may hold values from 6.7040493e-09 to 2.6816197e-08
- output_average: float32 [1024, 1024], P('mp', 'dp'), may hold values from -1.5 to 1.5
- gate_up_weight: float32 [2, 1024, 2752], P(None, 'dp', 'mp'), may hold values from -0.1875 to 0.1875
- gate_up_first: float32 [2, 1024, 2752], P(None, 'dp', 'mp'), may hold values from -0.0009765625 to 0.0009765625
- gate_up_second: float32 [2, 1024, 2752], P(None, 'dp', 'mp'), may hold values from 3.2775354e-08 to 1.3110142e-07
- gate_up_average: float32 [2, 1024, 2752], P(None, 'dp', 'mp'), may hold values from -0.1875 to 0.1875
- down_weight: float32 [2752, 1024], P('mp', 'dp'), may hold values from -0.109375 to 0.109375
- down_first: float32 [2752, 1024], P('mp', 'dp'), may hold values from -0.001953125 to 0.001953125
- down_second: float32 [2752, 1024], P('mp', 'dp'), may hold values from 1.0726479e-07 to 4.2905916e-07
- down_average: float32 [2752, 1024], P('mp', 'dp'), may hold values from -0.109375 to 0.109375
- gains: float32 [2, 1024], P(None, 'dp'), may hold values from 0.5 to 1.5
- gains_first: float32 [2, 1024], P(None, 'dp'), may hold values from -0.0034179688 to 0.0034179688
- gains_second: float32 [2, 1024], P(None, 'dp'), may hold values from 2.9795777e-07 to 1.1918311e-06
- gains_average: float32 [2, 1024], P(None, 'dp'), may hold values from 0.5 to 1.5
Outputs:
- block_out: bfloat16 [32768, 1024], P('dp', 'mp')
- input_grad: float32 [32768, 1024], P('dp', 'mp')
- grad_norm: float32 [], replicated
- qk_first_new: float32 [2, 1024, 256], P(None, 'dp')
- qk_second_new: float32 [2, 1024, 256], P(None, 'dp')
- qk_new: float32 [2, 1024, 256], P(None, 'dp')
- qk_average_new: float32 [2, 1024, 256], P(None, 'dp')
- value_first_new: float32 [1024, 1024], P('dp', 'mp')
- value_second_new: float32 [1024, 1024], P('dp', 'mp')
- value_new: float32 [1024, 1024], P('dp', 'mp')
- value_average_new: float32 [1024, 1024], P('dp', 'mp')
- output_first_new: float32 [1024, 1024], P('mp', 'dp')
- output_second_new: float32 [1024, 1024], P('mp', 'dp')
- output_new: float32 [1024, 1024], P('mp', 'dp')
- output_average_new: float32 [1024, 1024], P('mp', 'dp')
- gate_up_first_new: float32 [2, 1024, 2752], P(None, 'dp', 'mp')
- gate_up_second_new: float32 [2, 1024, 2752], P(None, 'dp', 'mp')
- gate_up_new: float32 [2, 1024, 2752], P(None, 'dp', 'mp')
- gate_up_average_new: float32 [2, 1024, 2752], P(None, 'dp', 'mp')
- down_first_new: float32 [2752, 1024], P('mp', 'dp')
- down_second_new: float32 [2752, 1024], P('mp', 'dp')
- down_new: float32 [2752, 1024], P('mp', 'dp')
- down_average_new: float32 [2752, 1024], P('mp', 'dp')
- gains_first_new: float32 [2, 1024], P(None, 'dp')
- gains_second_new: float32 [2, 1024], P(None, 'dp')
- gains_new: float32 [2, 1024], P(None, 'dp')
- gains_average_new: float32 [2, 1024], P(None, 'dp')
All inputs are finite; a program needn't handle non-finite values.
Results may differ from a plain program's by a relative error of at most 0.018.
Values may be sent and summed in bfloat16 or wider, within the bound.
A program may use at most 256 MiB of HBM per device.

v0:
```python
import math
import jax
import jax.numpy as jnp
from jax import lax
from jax.sharding import PartitionSpec as P

D = 1024
H = 16
F = 16
VH = 64
FF = 2752
V_ALL = 1024
LEN = 1024
STEP = 5


def inner(left, right):
    return lax.dot_general(
        left, right, (((0,), (0,)), ((), ())), preferred_element_type=jnp.float32
    )


def against(left, right):
    return lax.dot_general(
        left, right, (((1,), (1,)), ((), ())), preferred_element_type=jnp.float32
    )


def rms_scale(values):
    return lax.rsqrt(jnp.mean(values * values, axis=1, keepdims=True) + 1e-05)


def score_table(query, keys):
    length = query.shape[0]
    causal = (jnp.arange(length)[:, None] >= jnp.arange(length)[None, :]).astype(jnp.float32)
    tiled = jnp.einsum("ihf,jhf->hij", query, keys, preferred_element_type=jnp.float32) / math.sqrt(
        query.shape[2]
    )
    return (tiled, causal)


def mix_forward(parts):
    query, keys, values = parts
    tiled, causal = score_table(query, keys)
    kernel = causal * (1.0 + tiled + 0.5 * tiled * tiled)
    numer = jnp.einsum(
        "hij,jhv->ihv", kernel.astype(jnp.bfloat16), values, preferred_element_type=jnp.float32
    )
    return (numer, jnp.sum(kernel, axis=2).T)


def mix_backward(parts):
    query, keys, values, numer, denom, grad_mixed = parts
    tiled, causal = score_table(query, keys)
    kernel = causal * (1.0 + tiled + 0.5 * tiled * tiled)
    grad_numer = (grad_mixed / denom[:, :, None]).astype(jnp.bfloat16)
    grad_denom = -jnp.sum(grad_mixed * numer, axis=2) / (denom * denom)
    grad_kernel = (
        jnp.einsum("ihv,jhv->hij", grad_numer, values, preferred_element_type=jnp.float32)
        + grad_denom.T[:, :, None]
    )
    grad_tiled = (causal * grad_kernel * (1.0 + tiled)).astype(jnp.bfloat16)
    root = math.sqrt(query.shape[2])
    grad_values = jnp.einsum(
        "hij,ihv->jhv", kernel.astype(jnp.bfloat16), grad_numer, preferred_element_type=jnp.float32
    ).astype(jnp.bfloat16)
    grad_query = (
        jnp.einsum("hij,jhf->ihf", grad_tiled, keys, preferred_element_type=jnp.float32) / root
    ).astype(jnp.bfloat16)
    grad_keys = (
        jnp.einsum("hij,ihf->jhf", grad_tiled, query, preferred_element_type=jnp.float32) / root
    ).astype(jnp.bfloat16)
    return (grad_query, grad_keys, grad_values)


def adam_step(grad, first, second, weight, average, rate):
    first = 0.5 * first + 0.5 * grad
    second = 0.5 * second + 0.5 * grad * grad
    correct = 1.0 - 0.5**STEP
    weight = weight - rate * (first / correct / (jnp.sqrt(second / correct) + 1e-08) + 0.1 * weight)
    average = 0.5 * average + 0.5 * weight
    return (first, second, weight, average)


def on_device(
    tokens,
    out_grad,
    qk_weight,
    qk_first,
    qk_second,
    qk_average,
    value_weight,
    value_first,
    value_second,
    value_average,
    output_weight,
    output_first,
    output_second,
    output_average,
    gate_up_weight,
    gate_up_first,
    gate_up_second,
    gate_up_average,
    down_weight,
    down_first,
    down_second,
    down_average,
    gains,
    gains_first,
    gains_second,
    gains_average,
):
    groups = lax.axis_size("mp")
    rank = lax.axis_index("mp")
    qk_full, value_local, output_local, gate_up_local, down_local, gains_full = (
        lax.all_gather(qk_weight.astype(jnp.bfloat16), "dp", axis=1, tiled=True),
        lax.all_gather(value_weight.astype(jnp.bfloat16), "dp", axis=0, tiled=True),
        lax.all_gather(output_weight.astype(jnp.bfloat16), "dp", axis=1, tiled=True),
        lax.all_gather(gate_up_weight.astype(jnp.bfloat16), "dp", axis=1, tiled=True),
        lax.all_gather(down_weight.astype(jnp.bfloat16), "dp", axis=1, tiled=True),
        lax.all_gather(gains.astype(jnp.bfloat16), "dp", axis=1, tiled=True),
    )
    width = qk_full.shape[2] // groups
    qk_local = lax.dynamic_slice_in_dim(qk_full, rank * width, width, 2)
    tok_count = tokens.shape[0]
    seq_count = tok_count // LEN
    heads_here = H // groups
    cols = tokens.shape[1] // groups
    col_start = rank * cols
    first_gain = gains_full[0].astype(jnp.float32)
    second_gain = gains_full[1].astype(jnp.float32)
    inputs = tokens.astype(jnp.float32)
    scale_one = rms_scale(inputs)
    normed_one = inputs * scale_one
    hidden_one = (normed_one * first_gain).astype(jnp.bfloat16)
    query = jnp.dot(hidden_one, qk_local[0], preferred_element_type=jnp.float32).astype(
        jnp.bfloat16
    )
    keys = jnp.dot(hidden_one, qk_local[1], preferred_element_type=jnp.float32).astype(jnp.bfloat16)
    values = jnp.dot(hidden_one, value_local, preferred_element_type=jnp.float32).astype(
        jnp.bfloat16
    )
    head_query = query.reshape(seq_count, LEN, heads_here, F)
    head_keys = keys.reshape(seq_count, LEN, heads_here, F)
    head_values = values.reshape(seq_count, LEN, heads_here, VH)
    numer, denom = lax.map(mix_forward, (head_query, head_keys, head_values))
    mixed = (numer / denom[:, :, :, None]).astype(jnp.bfloat16).reshape(tok_count, heads_here * VH)
    attn_part = jnp.dot(mixed, output_local, preferred_element_type=jnp.float32)
    resid = inputs + lax.psum(attn_part.astype(jnp.bfloat16), "mp").astype(jnp.float32)
    scale_two = rms_scale(resid)
    normed_two = resid * scale_two
    hidden_two = (normed_two * second_gain).astype(jnp.bfloat16)
    gate = jnp.dot(hidden_two, gate_up_local[0], preferred_element_type=jnp.float32)
    lift = jnp.dot(hidden_two, gate_up_local[1], preferred_element_type=jnp.float32)
    sigma = jax.nn.sigmoid(gate)
    activ = (gate * sigma * lift).astype(jnp.bfloat16)
    down_part = jnp.dot(activ, down_local, preferred_element_type=jnp.float32)
    block_out = (
        lax.dynamic_slice_in_dim(resid, col_start, cols, 1)
        + lax.psum_scatter(
            down_part.astype(jnp.bfloat16), "mp", scatter_dimension=1, tiled=True
        ).astype(jnp.float32)
    ).astype(jnp.bfloat16)
    cotan = out_grad.astype(jnp.float32)
    grad_activ = against(out_grad, down_local)
    down_grad = inner(activ, out_grad)
    grad_gate = (grad_activ * lift * sigma * (1.0 + gate * (1.0 - sigma))).astype(jnp.bfloat16)
    grad_lift = (grad_activ * gate * sigma).astype(jnp.bfloat16)
    gate_up_grad = jnp.stack((inner(hidden_two, grad_gate), inner(hidden_two, grad_lift)))
    back_two = lax.psum(
        (against(grad_gate, gate_up_local[0]) + against(grad_lift, gate_up_local[1])).astype(
            jnp.bfloat16
        ),
        "mp",
    ).astype(jnp.float32)
    gain_two = jnp.sum(back_two * normed_two, axis=0)
    grad_resid = (
        cotan
        + scale_two * second_gain * back_two
        - resid * scale_two**3 * jnp.mean(resid * second_gain * back_two, axis=1, keepdims=True)
    )
    resid_low = grad_resid.astype(jnp.bfloat16)
    output_grad = inner(mixed, resid_low)
    grad_mixed = against(resid_low, output_local).reshape(seq_count, LEN, heads_here, VH)
    grad_query, grad_keys, grad_values = lax.map(
        mix_backward, (head_query, head_keys, head_values, numer, denom, grad_mixed)
    )
    grad_query = grad_query.reshape(tok_count, width)
    grad_keys = grad_keys.reshape(tok_count, width)
    grad_values = grad_values.reshape(tok_count, heads_here * VH)
    qk_grad = jnp.stack((inner(hidden_one, grad_query), inner(hidden_one, grad_keys)))
    value_grad = inner(hidden_one, grad_values)
    back_one = (
        against(grad_query, qk_local[0])
        + against(grad_keys, qk_local[1])
        + against(grad_values, value_local)
    )
    input_part = scale_one * first_gain * back_one - inputs * scale_one**3 * jnp.mean(
        inputs * first_gain * back_one, axis=1, keepdims=True
    )
    gains_grad = jnp.stack((jnp.sum(back_one * normed_one, axis=0), gain_two))
    input_grad = lax.dynamic_slice_in_dim(grad_resid, col_start, cols, 1) + lax.psum_scatter(
        input_part.astype(jnp.bfloat16), "mp", scatter_dimension=1, tiled=True
    ).astype(jnp.float32)
    qk_grad = lax.all_gather(qk_grad.astype(jnp.bfloat16), "mp", axis=2, tiled=True).astype(
        qk_grad.dtype
    )
    qk_share, value_share, output_share, gate_up_share, down_share, gains_share = (
        lax.psum_scatter(qk_grad, "dp", scatter_dimension=1, tiled=True),
        lax.psum_scatter(value_grad, "dp", scatter_dimension=0, tiled=True),
        lax.psum_scatter(output_grad, "dp", scatter_dimension=1, tiled=True),
        lax.psum_scatter(gate_up_grad, "dp", scatter_dimension=1, tiled=True),
        lax.psum_scatter(down_grad, "dp", scatter_dimension=1, tiled=True),
        lax.psum_scatter(gains_grad, "dp", scatter_dimension=1, tiled=True),
    )
    first_row = lax.psum(gains_share[0], "mp")
    gains_share = jnp.stack((first_row, gains_share[1]))
    spread_sum = (
        jnp.sum(value_share * value_share)
        + jnp.sum(output_share * output_share)
        + jnp.sum(gate_up_share * gate_up_share)
        + jnp.sum(down_share * down_share)
    )
    shared_sum = jnp.sum(qk_share * qk_share) + jnp.sum(gains_share * gains_share)
    total = lax.psum(spread_sum + shared_sum / groups, ("dp", "mp"))
    grad_norm = jnp.sqrt(total)
    clip = jnp.minimum(1.0, 1.0 / (grad_norm + 1e-06))
    qk_m, qk_v, qk_w, qk_a = adam_step(
        clip * qk_share, qk_first, qk_second, qk_weight, qk_average, 1.0 / math.sqrt(D)
    )
    value_m, value_v, value_w, value_a = adam_step(
        clip * value_share,
        value_first,
        value_second,
        value_weight,
        value_average,
        1.0 / math.sqrt(D),
    )
    output_m, output_v, output_w, output_a = adam_step(
        clip * output_share,
        output_first,
        output_second,
        output_weight,
        output_average,
        1.0 / math.sqrt(max(1, V_ALL * 16 // LEN)),
    )
    gate_up_m, gate_up_v, gate_up_w, gate_up_a = adam_step(
        clip * gate_up_share,
        gate_up_first,
        gate_up_second,
        gate_up_weight,
        gate_up_average,
        1.0 / math.sqrt(D),
    )
    down_m, down_v, down_w, down_a = adam_step(
        clip * down_share, down_first, down_second, down_weight, down_average, 1.0 / math.sqrt(FF)
    )
    gains_m, gains_v, gains_w, gains_a = adam_step(
        clip * gains_share, gains_first, gains_second, gains, gains_average, 0.4
    )
    return (
        block_out,
        input_grad,
        grad_norm,
        qk_m,
        qk_v,
        qk_w,
        qk_a,
        value_m,
        value_v,
        value_w,
        value_a,
        output_m,
        output_v,
        output_w,
        output_a,
        gate_up_m,
        gate_up_v,
        gate_up_w,
        gate_up_a,
        down_m,
        down_v,
        down_w,
        down_a,
        gains_m,
        gains_v,
        gains_w,
        gains_a,
    )


def solution(mesh):
    placed = (
        P("dp", None),
        P("dp", None),
        P(None, "dp", None),
        P(None, "dp", None),
        P(None, "dp", None),
        P(None, "dp", None),
        P("dp", "mp"),
        P("dp", "mp"),
        P("dp", "mp"),
        P("dp", "mp"),
        P("mp", "dp"),
        P("mp", "dp"),
        P("mp", "dp"),
        P("mp", "dp"),
        P(None, "dp", "mp"),
        P(None, "dp", "mp"),
        P(None, "dp", "mp"),
        P(None, "dp", "mp"),
        P("mp", "dp"),
        P("mp", "dp"),
        P("mp", "dp"),
        P("mp", "dp"),
        P(None, "dp"),
        P(None, "dp"),
        P(None, "dp"),
        P(None, "dp"),
    )
    return jax.shard_map(
        on_device,
        mesh=mesh,
        in_specs=placed,
        out_specs=(
            P("dp", "mp"),
            P("dp", "mp"),
            P(),
            P(None, "dp", None),
            P(None, "dp", None),
            P(None, "dp", None),
            P(None, "dp", None),
            P("dp", "mp"),
            P("dp", "mp"),
            P("dp", "mp"),
            P("dp", "mp"),
            P("mp", "dp"),
            P("mp", "dp"),
            P("mp", "dp"),
            P("mp", "dp"),
            P(None, "dp", "mp"),
            P(None, "dp", "mp"),
            P(None, "dp", "mp"),
            P(None, "dp", "mp"),
            P("mp", "dp"),
            P("mp", "dp"),
            P("mp", "dp"),
            P("mp", "dp"),
            P(None, "dp"),
            P(None, "dp"),
            P(None, "dp"),
            P(None, "dp"),
        ),
        check_vma=False,
    )
```

profile of v0, /device:TPU:0, one launch (start us, length us, event | category | flops | bytes accessed | tf_op | source)
XLA Modules:
  0.0 1489.0 jit_solution(11503148982517520819)
XLA Ops:
  9.9 22.2 %all_gather.21 = bf16[2,1024]{1,0:T(2,128)(2,1)S(1)} all-gather(bf16[2,128]{1,0:T(2,128)(2,1)S(1)} %convert_element_type.163), channel_id=1, replica_groups=mesh['dp'=8,'mp'=4] {'dp'}, dimensions={1}, use_global_device_ids=true | all-gather | bytes 4608 | tf_op jit(solution)/shard_map/all_gather | solution.py:121
  32.2 5.1 fusion.56
  37.9 31.9 %all_gather.22 = bf16[1024,256]{1,0:T(8,128)(2,1)S(1)} all-gather(bf16[128,256]{1,0:T(8,128)(2,1)S(1)} %convert_element_type.165), channel_id=1, replica_groups=mesh['dp'=8,'mp'=4] {'dp'}, dimensions={0}, use_global_device_ids=true | all-gather | bytes 589824 | tf_op jit(solution)/shard_map/all_gather | solution.py:117
  80.9 5.6 copy.95
  86.5 28.1 %all_gather.24 = bf16[256,1024]{1,0:T(8,128)(2,1)} all-gather(bf16[256,128]{1,0:T(8,128)(2,1)S(1)} %convert_element_type.171), channel_id=1, replica_groups=mesh['dp'=8,'mp'=4] {'dp'}, dimensions={1}, use_global_device_ids=true | all-gather | bytes 589824 | tf_op jit(solution)/shard_map/all_gather | solution.py:118
  114.6 6.1 convolution_convert_fusion.3
  121.3 6.1 convolution_convert_fusion.4
  129.8 35.0 %while.30 = (s32[]{:T(128)}, f32[4,1024,4,64]{1,3,2,0:T(8,128)}, f32[4,1024,4]{1,2,0:T(4,128)S(1)}, bf16[4,1024,4,64]{1,3,2,0:T(8,128)(2,1)S(1)}, bf16[4,1024,4,...) while((s32[]{:T(128)}, f32[4,1024,4,64]{1,3,2,0:T(8,128)}, ...), condition=%wide.region_3.4_spmd, body=%wide.region_1.3_spmd.sunk | while | flops 706736128 | bytes 27052120 | solution.py:146
  130.5 5.6 fusion.150
  139.2 5.6 fusion.150
  147.9 5.6 fusion.150
  156.6 5.6 fusion.150
  164.8 4.0 divide_convert_fusion.3
  172.6 5.7 convolution_convert_fusion.1
  181.0 148.5 %all-reduce.3.cloned.1.call-done = bf16[4096,1024]{1,0:T(8,128)(2,1)} async-done(((bf16[4096,1024]{1,0:T(8,128)(2,1)}), bf16[4096,1024]{1,0:T(8,128)(2,1)}) %all-reduce.3.cloned.1.call-update) | async-done | bytes 8388624 | tf_op jit(solution)/shard_map/psum | solution.py:149
  329.6 8.6 multiply_reduce_fusion
  338.1 10.8 multiply_convert_fusion.9
  348.9 42.7 %all-gather.7.cloned.1.call-done = bf16[2,1024,688]{1,2,0:T(8,128)(2,1)} async-done(((bf16[2,128,688]{1,2,0:T(8,128)(2,1)}), bf16[2,1024,688]{1,2,0:T(8,128)(2,1)}) %all-gather.7.cloned.1.call-update) | async-done | bytes 2818064 | tf_op jit(solution)/shard_map/all_gather | solution.py:119
  391.6 12.5 fusion.68
  404.1 8.8 fusion.67
  412.9 22.6 %all-gather.9.cloned.1.call-done = bf16[688,1024]{1,0:T(8,128)(2,1)} async-done(((bf16[688,128]{1,0:T(8,128)(2,1)}), bf16[688,1024]{1,0:T(8,128)(2,1)}) %all-gather.9.cloned.1.call-update) | async-done | bytes 1409040 | tf_op jit(solution)/shard_map/all_gather | solution.py:120
  435.5 22.1 %multiply_convert_fusion.10 = (bf16[4096,688]{0,1:T(8,128)(2,1)}, bf16[4096,688]{0,1:T(8,128)(2,1)}, bf16[4096,688]{0,1:T(8,128)(2,1)}) fusion(f32[4096,688]{0,1:T(8,128)} %fusion.67, f32[4096,688]{0,1:T(8,128)} %fusion.68, bf16[4096,1024]{1,0:T(8,128)(2,1)} %param.31, bf16[688,1024]{1,0:T(8,128)(2,1)} %all-gather.9.cloned.1.call-done), kind=kOutput, calls=%fused_computation.84 | convolution fusion | flops 5816451072 | bytes 49250304 | tf_op jit(solution)/shard_map/dot_general | solution.py:24
  457.6 13.2 fusion.66
  470.8 12.5 add_convert_fusion
  483.4 151.4 %all-reduce.5.cloned.1.call-done = bf16[4096,1024]{1,0:T(8,128)(2,1)} async-done(((bf16[4096,1024]{1,0:T(8,128)(2,1)}), bf16[4096,1024]{1,0:T(8,128)(2,1)}) %all-reduce.5.cloned.1.call-update) | async-done | bytes 8388624 | tf_op jit(solution)/shard_map/psum | solution.py:170
  634.8 12.0 fusion.55
  646.8 17.5 %fusion.53 = (f32[4096,1024]{1,0:T(8,128)S(1)}, f32[4096,1024]{1,0:T(8,128)}) fusion(bf16[4096,1024]{1,0:T(8,128)(2,1)} %all-reduce.5.cloned.1.call-done, bf16[4096,1024]{1,0:T(8,128)(2,1)} %param.31, f32[4096]{0:T(1024)S(1)} %broadcast_multiply_fusion.1, f32[4096]{0:T(1024)S(1)} %get-tuple-element.439, f32[1024]{0:T(1024)S(1)} %bitcast.225, ...), kind=kLoop, calls=%fused_computation.71 | loop fusion | flops 46137344 | bytes 67162112 | tf_op jit(solution)/shard_map/sub | solution.py:178
  664.3 5.7 copy-done.5
  670.1 4.4 fusion.64
  674.4 6.0 reshape.148
  680.5 141.2 %while.31 = (s32[]{:T(128)}, bf16[4,1024,4,16]{1,3,2,0:T(8,128)(2,1)}, bf16[4,1024,4,16]{1,3,2,0:T(8,128)(2,1)}, bf16[4,1024,4,64]{1,3,2,0:T(8,128)(2,1)}, bf16[...) while((s32[]{:T(128)}, ...), condition=%wide.region_11.12_spmd, body=%wide.region_9.11_spmd.sunk | while | flops 1535123456 | bytes 167644336 | solution.py:185
  690.7 5.7 copy-done
  696.4 4.8 fusion.165
  701.1 8.3 multiply_convert_fusion.16
  725.8 5.7 copy-done
  731.5 4.7 fusion.165
  736.3 8.3 multiply_convert_fusion.16
  761.0 5.7 copy-done
  766.7 4.7 fusion.165
  771.4 8.3 multiply_convert_fusion.16
  796.2 5.7 copy-done
  801.9 4.7 fusion.165
  806.6 8.3 multiply_convert_fusion.16
  832.6 9.6 fusion.75
  842.3 9.3 fusion.74
  851.6 18.5 %fusion.51 = (f32[1024]{0:T(1024)S(1)}, f32[4096]{0:T(1024)S(1)}, f32[4096,1024]{1,0:T(8,128)}) fusion(bf16[4096,1024]{1,0:T(8,128)(2,1)S(1)} %bitcast.205, f32[4096]{0:T(1024)S(1)} %copy-done.29, f32[1024]{0:T(1024)S(1)} %bitcast.221, bf16[4096,256]{0,1:T(8,128)(2,1)S(1)} %bitcast.208, bf16[1024,256]{1,0:T(8,128)(2,1)} %copy-done.19, ...), kind=kOutput, calls=%fused_computation.69 | convolution fusion | flops 2185227264 | bytes 61382656 | tf_op jit(solution)/shard_map/dot_general | solution.py:24
  871.2 11.6 fusion.92
  882.9 9.2 fusion.62
  892.1 7.4 fusion.91
  902.5 10.3 convolution_bitcast_fusion
  912.8 10.1 convolution_bitcast_fusion.1
  926.0 11.8 convolution_convert_fusion
  938.5 12.5 fusion.59
  953.7 6.1 psum.30
  960.4 50.7 %reduce-scatter.21.cloned.1.call-done = f32[688,128]{1,0:T(8,128)} async-done(((f32[688,1024]{1,0:T(8,128)}), f32[688,128]{1,0:T(8,128)}) %reduce-scatter.21.cloned.1.call-update) | async-done | bytes 352272 | tf_op jit(solution)/shard_map/reduce_scatter | solution.py:213
  1012.9 64.5 %reduce-scatter.17.cloned.1.call-done = f32[256,128]{1,0:T(8,128)} async-done(((f32[256,1024]{1,0:T(8,128)}), f32[256,128]{1,0:T(8,128)}) %reduce-scatter.17.cloned.1.call-update) | async-done | bytes 131088 | tf_op jit(solution)/shard_map/reduce_scatter | solution.py:211
  1078.9 64.1 %reduce-scatter.15.cloned.1.call-done = f32[128,256]{1,0:T(8,128)} async-done(((f32[1024,256]{1,0:T(8,128)}), f32[128,256]{1,0:T(8,128)}) %reduce-scatter.15.cloned.1.call-update) | async-done | bytes 131088 | tf_op jit(solution)/shard_map/reduce_scatter | solution.py:210
  1145.9 69.1 %reduce-scatter.23.cloned.1.call-done = f32[2,128,256]{1,2,0:T(8,128)} async-done(((f32[2,1024,256]{1,2,0:T(8,128)}), f32[2,128,256]{1,2,0:T(8,128)}) %reduce-scatter.23.cloned.1.call-update) | async-done | bytes 262160 | tf_op jit(solution)/shard_map/reduce_scatter | solution.py:209
  1217.9 108.5 %reduce-scatter.19.cloned.1.call-done = f32[2,128,688]{1,2,0:T(8,128)} async-done(((f32[2,1024,688]{1,2,0:T(8,128)}), f32[2,128,688]{1,2,0:T(8,128)}) %reduce-scatter.19.cloned.1.call-update) | async-done | bytes 704528 | tf_op jit(solution)/shard_map/reduce_scatter | solution.py:212
  1329.7 40.8 %psum.31 = f32[]{:T(128)} all-reduce(f32[]{:T(128)S(6)} %add.280), channel_id=1, replica_groups=mesh['dp'=8,'mp'=4] {'dp','mp'}, use_global_device_ids=true, to_apply=%region_29.30 | all-reduce | flops 1 | bytes 8 | tf_op jit(solution)/shard_map/psum | solution.py:225
  1390.8 10.6 reduce-scatter.11.cloned.1.call-done
  1401.4 4.6 add_convert_fusion.1
  1406.0 69.6 %reduce-scatter.13.cloned.1.call-done = bf16[4096,256]{1,0:T(8,128)(2,1)} async-done(((bf16[4096,1024]{1,0:T(8,128)(2,1)}), bf16[4096,256]{1,0:T(8,128)(2,1)}) %reduce-scatter.13.cloned.1.call-update) | async-done | bytes 2097168 | tf_op jit(solution)/shard_map/reduce_scatter | solution.py:202
  1475.6 5.2 convert_add_fusion.1
  (230 shorter events, 151.4 us)
Async XLA Ops:
  7.2 30.7 %copy-start.24 = (f32[128,256]{1,0:T(8,128)S(1)}, f32[128,256]{1,0:T(8,128)}, u32[]{:S(2)}) copy-start(f32[128,256]{1,0:T(8,128)} %param.36) | copy-start | bytes 393220
  7.2 30.7 %copy-start.26 = (f32[256,128]{1,0:T(8,128)S(1)}, f32[256,128]{1,0:T(8,128)}, u32[]{:S(2)}) copy-start(f32[256,128]{1,0:T(8,128)} %param.40) | copy-start | bytes 393220
  7.2 107.4 %all-gather.5.cloned.1.call-start = ((), (), s32[]{:S(2)}) async-start(), calls=%async_computation.8 | async-start | bytes 1179648 | tf_op jit(solution)/shard_map/all_gather | solution.py:116
  9.0 320.6 %all-reduce.3.cloned.1.call-start = ((), (), s32[]{:S(2)}) async-start(), calls=%async_computation.9 | async-start | bytes 16777216 | tf_op jit(solution)/shard_map/psum | solution.py:149
  9.0 60.8 %copy-start.1 = (bf16[4096,1024]{1,0:T(8,128)(2,1)S(1)}, bf16[4096,1024]{1,0:T(8,128)(2,1)}, u32[]{:S(2)}) copy-start(bf16[4096,1024]{1,0:T(8,128)(2,1)} %param.30) | copy-start | bytes 25165828
  32.2 40.0 %copy-start.34 = (f32[1,1024]{1,0:T(1,128)}, f32[1,1024]{1,0:T(1,128)S(1)}, u32[]{:S(2)}) copy-start(f32[1,1024]{1,0:T(1,128)S(1)} %get-tuple-element.441) | copy-start | bytes 12292
  37.9 32.0 %copy-start.28 = (f32[4096]{0:T(1024)}, f32[4096]{0:T(1024)S(1)}, u32[]{:S(2)}) copy-start(f32[4096]{0:T(1024)S(1)} %get-tuple-element.438) | copy-start | bytes 49156
  69.9 2.3 copy-start.19
  72.1 3.2 copy-start.2
  164.8 6.5 copy-start.30
  164.8 13.5 copy-start.6
  164.8 13.5 copy-start.12
  164.8 13.5 copy-start.13
  164.8 7.8 copy-start.14
  171.3 1.3 copy-start.7
  178.3 2.0 copy-start.20
  178.3 1.2 copy-start.16
  178.3 213.3 %all-gather.7.cloned.1.call-start = ((), (), s32[]{:S(2)}) async-start(), calls=%async_computation.10 | async-start | bytes 3170304 | tf_op jit(solution)/shard_map/all_gather | solution.py:119
  180.2 255.3 %all-gather.9.cloned.1.call-start = ((), (), s32[]{:S(2)}) async-start(), calls=%async_computation.11 | async-start | bytes 1585152 | tf_op jit(solution)/shard_map/all_gather | solution.py:120
  181.0 453.8 %all-reduce.5.cloned.1.call-start = ((), (), s32[]{:S(2)}) async-start(), calls=%async_computation.13 | async-start | bytes 16777216 | tf_op jit(solution)/shard_map/psum | solution.py:170
  391.6 12.5 copy-start.10
  391.6 12.5 copy-start.40
  457.6 13.2 copy-start.42
  483.3 416.3 %all-gather.11.cloned.1.call-start = ((), (), s32[]{:S(2)}) async-start(), calls=%async_computation.19 | async-start | bytes 1310720 | tf_op jit(solution)/shard_map/all_gather | solution.py:205
  646.8 23.2 %copy-start.15 = (bf16[256,1024]{1,0:T(8,128)(2,1)S(1)}, bf16[256,1024]{1,0:T(8,128)(2,1)}, u32[]{:S(2)}) copy-start(bf16[256,1024]{1,0:T(8,128)(2,1)} %all_gather.24) | copy-start | bytes 1572868
  664.3 5.7 copy-start.5
  684.1 6.5 copy-start.4
  690.6 5.7 copy-start
  719.3 6.5 copy-start.4
  725.8 5.7 copy-start
  754.5 6.5 copy-start.4
  761.0 5.7 copy-start
  789.6 6.5 copy-start.4
  796.2 5.7 copy-start
  821.7 6.3 copy-start.3
  825.9 25.6 %copy-start.9 = (bf16[32,8,4,1024]{3,1,2,0:T(8,128)(2,1)}, bf16[32,8,4,1024]{3,1,2,0:T(8,128)(2,1)S(1)}, u32[]{:S(2)}) copy-start(bf16[32,8,4,1024]{3,1,2,0:T(8,128)(2,1)S(1)} %copy.128) | copy-start | bytes 6291460
  828.0 1.6 copy-start.27
  830.2 1.6 copy-start.11
  832.6 120.0 %reduce-scatter.25.cloned.1.call-start = ((), (), s32[]{:S(2)}) async-start(), calls=%async_computation.21 | async-start | bytes 589824
  832.6 18.9 %slice-start = ((s8[8388608]{0:T(1024)(128)(4,1)}), s8[4194304]{0:T(1024)(128)(4,1)S(1)}, s32[]{:S(2)}) async-start(s8[8388608]{0:T(1024)(128)(4,1)} %bitcast.204), calls=%async_computation.22 | async-start | bytes 8388608
  842.3 9.3 slice-start.1
  842.3 9.3 copy-start.29
  842.3 9.3 copy-start.35
  851.6 18.5 %copy-start.37 = (f32[1024]{0:T(1024)S(1)}, f32[1024]{0:T(1024)}, u32[]{:S(2)}) copy-start(f32[1024]{0:T(1024)} %get-tuple-element.368) | copy-start | bytes 12292
  871.1 140.0 %reduce-scatter.21.cloned.1.call-start = ((), (), s32[]{:S(2)}) async-start(), calls=%async_computation.18 | async-start | bytes 3170304 | tf_op jit(solution)/shard_map/reduce_scatter | solution.py:213
  871.2 11.7 copy-start.8
  882.9 194.5 %reduce-scatter.17.cloned.1.call-start = ((), (), s32[]{:S(2)}) async-start(), calls=%async_computation.16 | async-start | bytes 1179648 | tf_op jit(solution)/shard_map/reduce_scatter | solution.py:211
  892.1 250.9 %reduce-scatter.15.cloned.1.call-start = ((), (), s32[]{:S(2)}) async-start(), calls=%async_computation.15 | async-start | bytes 1179648 | tf_op jit(solution)/shard_map/reduce_scatter | solution.py:210
  899.6 315.4 %reduce-scatter.23.cloned.1.call-start = ((), (), s32[]{:S(2)}) async-start(), calls=%async_computation.20 | async-start | bytes 2359296 | tf_op jit(solution)/shard_map/reduce_scatter | solution.py:209
  902.5 423.9 %reduce-scatter.19.cloned.1.call-start = ((), (), s32[]{:S(2)}) async-start(), calls=%async_computation.17 | async-start | bytes 6340608 | tf_op jit(solution)/shard_map/reduce_scatter | solution.py:212
  922.9 3.1 copy-start.41
  926.0 475.4 %reduce-scatter.11.cloned.1.call-start = ((), (), s32[]{:S(2)}) async-start(), calls=%async_computation.12 | async-start | bytes 10485760 | tf_op jit(solution)/shard_map/reduce_scatter | solution.py:160
  937.8 537.8 %reduce-scatter.13.cloned.1.call-start = ((), (), s32[]{:S(2)}) async-start(), calls=%async_computation.14 | async-start | bytes 10485760 | tf_op jit(solution)/shard_map/reduce_scatter | solution.py:202
  951.0 0.9 copy-start.23
  951.0 1.1 copy-start.31
  951.0 1.2 copy-start.32
  951.0 1.4 copy-start.33
  951.0 429.8 %copy-start.25 = (f32[128,256]{1,0:T(8,128)S(1)}, f32[128,256]{1,0:T(8,128)}, u32[]{:S(2)}) copy-start(f32[128,256]{1,0:T(8,128)} %param.36) | copy-start | bytes 393220
  951.1 433.7 %copy-start.21 = (f32[688,128]{1,0:T(8,128)S(1)}, f32[688,128]{1,0:T(8,128)}, u32[]{:S(2)}) copy-start(f32[688,128]{1,0:T(8,128)} %param.48) | copy-start | bytes 1056772
  951.1 436.2 %copy-start.17 = (f32[2,128,688]{1,2,0:T(8,128)S(1)}, f32[2,128,688]{1,2,0:T(8,128)}, u32[]{:S(2)}) copy-start(f32[2,128,688]{1,2,0:T(8,128)} %param.44) | copy-start | bytes 2113540
  953.7 417.5 %copy-start.38 = (f32[1,128]{1,0:T(1,128)}, f32[1,128]{1,0:T(1,128)S(1)}, u32[]{:S(2)}) copy-start(f32[1,128]{1,0:T(1,128)S(1)} %copy.124) | copy-start | bytes 1540
  959.8 411.4 %copy-start.39 = (f32[1,128]{1,0:T(1,128)}, f32[1,128]{1,0:T(1,128)S(1)}, u32[]{:S(2)}) copy-start(f32[1,128]{1,0:T(1,128)S(1)} %psum.30) | copy-start | bytes 1540
  1011.1 373.6 %copy-start.22 = (f32[688,128]{1,0:T(8,128)S(1)}, f32[688,128]{1,0:T(8,128)}, u32[]{:S(2)}) copy-start(f32[688,128]{1,0:T(8,128)} %reduce-scatter.21.cloned.1.call-done) | copy-start | bytes 1056772
  1326.4 60.9 %copy-start.18 = (f32[2,128,688]{1,2,0:T(8,128)S(1)}, f32[2,128,688]{1,2,0:T(8,128)}, u32[]{:S(2)}) copy-start(f32[2,128,688]{1,2,0:T(8,128)} %reduce-scatter.19.cloned.1.call-done) | copy-start | bytes 2113540
  (1 other events, 0.7 us)
Sparse Core Ops, SparseCore 0:
  10.8 46.0 all-gather.4
  178.4 151.0 all-reduce.2
  332.2 59.3 all-gather.6
  394.1 41.3 all-gather.8
  483.5 151.3 all-reduce.4
  832.7 16.8 all-gather.10
  871.3 62.0 reduce-scatter.24
  937.9 73.2 reduce-scatter.20
  1014.9 62.3 reduce-scatter.16
  1080.6 62.3 reduce-scatter.14
  1147.6 67.3 reduce-scatter.22
  1218.9 107.4 reduce-scatter.18
  1329.2 72.2 reduce-scatter.10
  1403.8 71.7 reduce-scatter.12
where the time goes:
time: 1500 us; the launch traced here: 1490 us
  waiting for transfers between devices  802 us (53%)
  matrix products  319 us (21%)
  other arithmetic  131 us (9%)
  blocking collectives  129 us (9%)
  local copies, waits for them, and re-layouts  84.8 us (6%)
  between operations  20.9 us (1%)
    psum x1, waiting for transfers between devices, on_device(): lax.psum((against(grad_gate, gate_up_local[0]) + against(grad_lift, gate_...  151 us
    psum x1, waiting for transfers between devices, on_device(): lax.psum(attn_part.astype(jnp.bfloat16), 'mp').astype(jnp.float32)  149 us
    reduce_scatter x1, waiting for transfers between devices, on_device(): lax.psum_scatter(gate_up_grad, 'dp', scatter_dimension=1, tiled=True)  108 us
    dot_general x7, matrix products, against(): lax.dot_general(left, right, (((1,), (1,)), ((), ())), preferred_element_...  89.6 us
    reduce_scatter x1, waiting for transfers between devices, on_device(): lax.psum_scatter(input_part.astype(jnp.bfloat16), 'mp', scatter_dimension...  69.6 us
    reduce_scatter x1, waiting for transfers between devices, on_device(): lax.psum_scatter(qk_grad, 'dp', scatter_dimension=1, tiled=True)  69.1 us
    reduce_scatter x1, waiting for transfers between devices, on_device(): lax.psum_scatter(output_grad, 'dp', scatter_dimension=1, tiled=True)  64.5 us
    reduce_scatter x1, waiting for transfers between devices, on_device(): lax.psum_scatter(value_grad, 'dp', scatter_dimension=0, tiled=True)  64.1 us
  transfers between devices with their start and end apart: 14, of which 11 were waited for; matrix products, arithmetic and copies ran while one was open for 14% of the time, Pallas kernels for 0%

commit v1 on v0

--- a/solution.py
+++ b/solution.py
@@ -1,3 +1,4 @@
+import functools
 import math
 import jax
 import jax.numpy as jnp
@@ -12,6 +13,14 @@
 V_ALL = 1024
 LEN = 1024
 STEP = 5
+
+
+def pack_cubes(q_in, device_axis):
+    tall = jax.lax.all_gather(q_in, device_axis)
+    return jnp.sum(tall, axis=0)
+
+
+do_the_words = functools.partial(pack_cubes, device_axis="mp")
 
 
 def inner(left, right):
@@ -146,7 +155,7 @@
     numer, denom = lax.map(mix_forward, (head_query, head_keys, head_values))
     mixed = (numer / denom[:, :, :, None]).astype(jnp.bfloat16).reshape(tok_count, heads_here * VH)
     attn_part = jnp.dot(mixed, output_local, preferred_element_type=jnp.float32)
-    resid = inputs + lax.psum(attn_part.astype(jnp.bfloat16), "mp").astype(jnp.float32)
+    resid = inputs + do_the_words(attn_part.astype(jnp.bfloat16)).astype(jnp.float32)
     scale_two = rms_scale(resid)
     normed_two = resid * scale_two
     hidden_two = (normed_two * second_gain).astype(jnp.bfloat16)

time: 1500 us -> 1550 us (1.033)
  waiting for transfers between devices: 802 us -> 833 us
  other arithmetic: 131 us -> 147 us
    all_gather x0 -> x1, waiting for transfers between devices: none -> 197 us  [pack_cubes(): tall = jax.lax.all_gather(q_in, device_axis)]
    psum x1 -> x0, waiting for transfers between devices: 149 us -> none  [on_device(): lax.psum(attn_part.astype(jnp.bfloat16), 'mp').astype(jnp.float32)]
    reduce_sum x0 -> x1, other arithmetic: none -> 17.2 us  [pack_cubes(): return jnp.sum(tall, axis=0)]
    all_gather x1, waiting for transfers between devices: 42.7 us -> 25.9 us  [on_device(): lax.all_gather(gate_up_weight.astype(jnp.bfloat16), 'dp', axis=1, tiled=T...]
  transfers between devices with their start and end apart: 14 -> 14, of which waited for: 11 -> 11; matrix products, arithmetic and copies ran while one was open for 14% -> 15% of each run, Pallas kernels for 0% -> 0%
where the time goes in v1:
time: 1550 us; the launch traced here: 1540 us
  waiting for transfers between devices  833 us (54%)
  matrix products  319 us (21%)
  other arithmetic  147 us (9%)
  blocking collectives  129 us (8%)
  local copies, waits for them, and re-layouts  84.8 us (5%)
  between operations  20.9 us (1%)
    all_gather x1, waiting for transfers between devices, pack_cubes(): tall = jax.lax.all_gather(q_in, device_axis)  197 us
    psum x1, waiting for transfers between devices, on_device(): lax.psum((against(grad_gate, gate_up_local[0]) + against(grad_lift, gate_...  151 us
    reduce_scatter x1, waiting for transfers between devices, on_device(): lax.psum_scatter(gate_up_grad, 'dp', scatter_dimension=1, tiled=True)  109 us
    dot_general x7, matrix products, against(): lax.dot_general(left, right, (((1,), (1,)), ((), ())), preferred_element_...  89.7 us
    reduce_scatter x1, waiting for transfers between devices, on_device(): lax.psum_scatter(input_part.astype(jnp.bfloat16), 'mp', scatter_dimension...  69.6 us
    reduce_scatter x1, waiting for transfers between devices, on_device(): lax.psum_scatter(qk_grad, 'dp', scatter_dimension=1, tiled=True)  68.8 us
    reduce_scatter x1, waiting for transfers between devices, on_device(): lax.psum_scatter(output_grad, 'dp', scatter_dimension=1, tiled=True)  64.5 us
    reduce_scatter x1, waiting for transfers between devices, on_device(): lax.psum_scatter(value_grad, 'dp', scatter_dimension=0, tiled=True)  64 us
  transfers between devices with their start and end apart: 14, of which 11 were waited for; matrix products, arithmetic and copies ran while one was open for 15% of the time, Pallas kernels for 0%

profile of v1, /device:TPU:0, one launch (start us, length us, event | category | flops | bytes accessed | tf_op | source)
XLA Modules:
  0.0 1536.3 jit_solution(3107563501415771057)
XLA Ops:
  9.9 22.2 %all_gather.27 = bf16[2,1024]{1,0:T(2,128)(2,1)S(1)} all-gather(bf16[2,128]{1,0:T(2,128)(2,1)S(1)} %convert_element_type.165), channel_id=1, replica_groups=mesh['dp'=8,'mp'=4] {'dp'}, dimensions={1}, use_global_device_ids=true | all-gather | bytes 4608 | tf_op jit(solution)/shard_map/all_gather | solution.py:130
  32.2 5.1 fusion.56
  37.9 31.9 %all_gather.28 = bf16[1024,256]{1,0:T(8,128)(2,1)S(1)} all-gather(bf16[128,256]{1,0:T(8,128)(2,1)S(1)} %convert_element_type.167), channel_id=1, replica_groups=mesh['dp'=8,'mp'=4] {'dp'}, dimensions={0}, use_global_device_ids=true | all-gather | bytes 589824 | tf_op jit(solution)/shard_map/all_gather | solution.py:126
  80.9 5.6 copy.95
  86.5 28.1 %all_gather.30 = bf16[256,1024]{1,0:T(8,128)(2,1)} all-gather(bf16[256,128]{1,0:T(8,128)(2,1)S(1)} %convert_element_type.173), channel_id=1, replica_groups=mesh['dp'=8,'mp'=4] {'dp'}, dimensions={1}, use_global_device_ids=true | all-gather | bytes 589824 | tf_op jit(solution)/shard_map/all_gather | solution.py:127
  114.6 6.1 convolution_convert_fusion.3
  121.3 6.1 convolution_convert_fusion.4
  129.8 35.0 %while.30 = (s32[]{:T(128)}, f32[4,1024,4,64]{1,3,2,0:T(8,128)}, f32[4,1024,4]{1,2,0:T(4,128)S(1)}, bf16[4,1024,4,64]{1,3,2,0:T(8,128)(2,1)S(1)}, bf16[4,1024,4,...) while((s32[]{:T(128)}, f32[4,1024,4,64]{1,3,2,0:T(8,128)}, ...), condition=%wide.region_3.4_spmd, body=%wide.region_1.3_spmd.sunk | while | flops 706736128 | bytes 27052120 | solution.py:155
  130.5 5.6 fusion.150
  139.2 5.6 fusion.150
  147.9 5.6 fusion.150
  156.6 5.6 fusion.150
  172.6 5.6 convolution_convert_fusion.1
  181.0 197.0 %all-gather.15.cloned.1.call-done = bf16[16384,1024]{1,0:T(8,128)(2,1)} async-done(((bf16[4096,1024]{1,0:T(8,128)(2,1)}), bf16[16384,1024]{1,0:T(8,128)(2,1)}) %all-gather.15.cloned.1.call-update) | async-done | bytes 33554448 | tf_op jit(solution)/shard_map/all_gather | solution.py:19
  378.1 17.2 %reduce_sum.145 = bf16[4096,1024]{1,0:T(8,128)(2,1)} reduce(bf16[4,4096,1024]{2,1,0:T(8,128)(2,1)} %bitcast.207, bf16[]{:T(256)} %constant.172.clone.1), dimensions={0}, to_apply=%region_4.5 | reduce | flops 12582912 | bytes 41943040 | tf_op jit(solution)/shard_map/reduce_sum | solution.py:20
  395.3 8.6 multiply_reduce_fusion
  403.9 10.1 multiply_convert_fusion.9
  414.0 25.9 %all-gather.9.cloned.1.call-done = bf16[2,1024,688]{1,2,0:T(8,128)(2,1)} async-done(((bf16[2,128,688]{1,2,0:T(8,128)(2,1)}), bf16[2,1024,688]{1,2,0:T(8,128)(2,1)}) %all-gather.9.cloned.1.call-update) | async-done | bytes 2818064 | tf_op jit(solution)/shard_map/all_gather | solution.py:128
  439.9 12.5 fusion.68
  452.4 8.8 fusion.67
  461.3 22.5 %all-gather.11.cloned.1.call-done = bf16[688,1024]{1,0:T(8,128)(2,1)} async-done(((bf16[688,128]{1,0:T(8,128)(2,1)}), bf16[688,1024]{1,0:T(8,128)(2,1)}) %all-gather.11.cloned.1.call-update) | async-done | bytes 1409040 | tf_op jit(solution)/shard_map/all_gather | solution.py:129
  483.8 22.3 %multiply_convert_fusion.10 = (bf16[4096,688]{0,1:T(8,128)(2,1)}, bf16[4096,688]{0,1:T(8,128)(2,1)}, bf16[4096,688]{0,1:T(8,128)(2,1)}) fusion(f32[4096,688]{0,1:T(8,128)} %fusion.67, f32[4096,688]{0,1:T(8,128)} %fusion.68, bf16[4096,1024]{1,0:T(8,128)(2,1)} %param.31, bf16[688,1024]{1,0:T(8,128)(2,1)} %all-gather.11.cloned.1.call-done), kind=kOutput, calls=%fused_computation.84 | convolution fusion | flops 5816451072 | bytes 49250304 | tf_op jit(solution)/shard_map/dot_general | solution.py:33
  506.1 13.0 fusion.66
  519.2 12.5 add_convert_fusion
  531.8 151.4 %all-reduce.2.cloned.1.call-done = bf16[4096,1024]{1,0:T(8,128)(2,1)} async-done(((bf16[4096,1024]{1,0:T(8,128)(2,1)}), bf16[4096,1024]{1,0:T(8,128)(2,1)}) %all-reduce.2.cloned.1.call-update) | async-done | bytes 8388624 | tf_op jit(solution)/shard_map/psum | solution.py:179
  683.2 12.0 fusion.55
  695.2 17.5 %fusion.53 = (f32[4096,1024]{1,0:T(8,128)S(1)}, f32[4096,1024]{1,0:T(8,128)}) fusion(bf16[4096,1024]{1,0:T(8,128)(2,1)} %all-reduce.2.cloned.1.call-done, bf16[4096,1024]{1,0:T(8,128)(2,1)} %param.31, f32[4096]{0:T(1024)S(1)} %broadcast_multiply_fusion.1, f32[4096]{0:T(1024)S(1)} %get-tuple-element.439, f32[1024]{0:T(1024)S(1)} %bitcast.227, ...), kind=kLoop, calls=%fused_computation.71 | loop fusion | flops 46137344 | bytes 67162112 | tf_op jit(solution)/shard_map/sub | solution.py:187
  712.7 5.7 copy-done.5
  718.5 4.4 fusion.64
  722.8 6.0 reshape.148
  728.9 141.2 %while.31 = (s32[]{:T(128)}, bf16[4,1024,4,16]{1,3,2,0:T(8,128)(2,1)}, bf16[4,1024,4,16]{1,3,2,0:T(8,128)(2,1)}, bf16[4,1024,4,64]{1,3,2,0:T(8,128)(2,1)}, bf16[...) while((s32[]{:T(128)}, ...), condition=%wide.region_11.12_spmd, body=%wide.region_9.11_spmd.sunk | while | flops 1535123456 | bytes 167644336 | solution.py:194
  739.1 5.7 copy-done
  744.8 4.8 fusion.165
  749.5 8.3 multiply_convert_fusion.16
  774.2 5.7 copy-done
  779.9 4.7 fusion.165
  784.7 8.3 multiply_convert_fusion.16
  809.4 5.7 copy-done
  815.1 4.7 fusion.165
  819.9 8.3 multiply_convert_fusion.16
  844.6 5.7 copy-done
  850.3 4.7 fusion.165
  855.0 8.3 multiply_convert_fusion.16
  881.0 9.6 fusion.75
  890.7 9.3 fusion.74
  900.0 18.5 %fusion.51 = (f32[1024]{0:T(1024)S(1)}, f32[4096]{0:T(1024)S(1)}, f32[4096,1024]{1,0:T(8,128)}) fusion(bf16[4096,1024]{1,0:T(8,128)(2,1)S(1)} %bitcast.206, f32[4096]{0:T(1024)S(1)} %copy-done.29, f32[1024]{0:T(1024)S(1)} %bitcast.223, bf16[4096,256]{0,1:T(8,128)(2,1)S(1)} %bitcast.210, bf16[1024,256]{1,0:T(8,128)(2,1)} %copy-done.19, ...), kind=kOutput, calls=%fused_computation.69 | convolution fusion | flops 2185227264 | bytes 61382656 | tf_op jit(solution)/shard_map/dot_general | solution.py:33
  919.6 11.6 fusion.92
  931.3 9.2 fusion.62
  940.6 7.4 fusion.91
  950.9 10.3 convolution_bitcast_fusion
  961.2 10.1 convolution_bitcast_fusion.1
  974.4 11.8 convolution_convert_fusion
  986.9 12.5 fusion.59
  1002.1 6.1 psum.22
  1008.8 49.8 %reduce-scatter.21.cloned.1.call-done = f32[688,128]{1,0:T(8,128)} async-done(((f32[688,1024]{1,0:T(8,128)}), f32[688,128]{1,0:T(8,128)}) %reduce-scatter.21.cloned.1.call-update) | async-done | bytes 352272 | tf_op jit(solution)/shard_map/reduce_scatter | solution.py:222
  1060.4 64.5 %reduce-scatter.17.cloned.1.call-done = f32[256,128]{1,0:T(8,128)} async-done(((f32[256,1024]{1,0:T(8,128)}), f32[256,128]{1,0:T(8,128)}) %reduce-scatter.17.cloned.1.call-update) | async-done | bytes 131088 | tf_op jit(solution)/shard_map/reduce_scatter | solution.py:220
  1126.4 64.0 %reduce-scatter.15.cloned.1.call-done = f32[128,256]{1,0:T(8,128)} async-done(((f32[1024,256]{1,0:T(8,128)}), f32[128,256]{1,0:T(8,128)}) %reduce-scatter.15.cloned.1.call-update) | async-done | bytes 131088 | tf_op jit(solution)/shard_map/reduce_scatter | solution.py:219
  1193.3 68.8 %reduce-scatter.23.cloned.1.call-done = f32[2,128,256]{1,2,0:T(8,128)} async-done(((f32[2,1024,256]{1,2,0:T(8,128)}), f32[2,128,256]{1,2,0:T(8,128)}) %reduce-scatter.23.cloned.1.call-update) | async-done | bytes 262160 | tf_op jit(solution)/shard_map/reduce_scatter | solution.py:218
  1265.1 108.6 %reduce-scatter.19.cloned.1.call-done = f32[2,128,688]{1,2,0:T(8,128)} async-done(((f32[2,1024,688]{1,2,0:T(8,128)}), f32[2,128,688]{1,2,0:T(8,128)}) %reduce-scatter.19.cloned.1.call-update) | async-done | bytes 704528 | tf_op jit(solution)/shard_map/reduce_scatter | solution.py:221
  1377.0 40.7 %psum.23 = f32[]{:T(128)} all-reduce(f32[]{:T(128)S(6)} %add.278), channel_id=1, replica_groups=mesh['dp'=8,'mp'=4] {'dp','mp'}, use_global_device_ids=true, to_apply=%region_29.30 | all-reduce | flops 1 | bytes 8 | tf_op jit(solution)/shard_map/psum | solution.py:234
  1438.1 10.7 reduce-scatter.11.cloned.1.call-done
  1448.7 4.6 add_convert_fusion.1
  1453.4 69.6 %reduce-scatter.13.cloned.1.call-done = bf16[4096,256]{1,0:T(8,128)(2,1)} async-done(((bf16[4096,1024]{1,0:T(8,128)(2,1)}), bf16[4096,256]{1,0:T(8,128)(2,1)}) %reduce-scatter.13.cloned.1.call-update) | async-done | bytes 2097168 | tf_op jit(solution)/shard_map/reduce_scatter | solution.py:211
  1522.9 5.2 convert_add_fusion.1
  (231 shorter events, 155.4 us)
Async XLA Ops:
  7.2 30.7 %copy-start.24 = (f32[128,256]{1,0:T(8,128)S(1)}, f32[128,256]{1,0:T(8,128)}, u32[]{:S(2)}) copy-start(f32[128,256]{1,0:T(8,128)} %param.36) | copy-start | bytes 393220
  7.2 30.7 %copy-start.26 = (f32[256,128]{1,0:T(8,128)S(1)}, f32[256,128]{1,0:T(8,128)}, u32[]{:S(2)}) copy-start(f32[256,128]{1,0:T(8,128)} %param.40) | copy-start | bytes 393220
  7.2 107.4 %all-gather.7.cloned.1.call-start = ((), (), s32[]{:S(2)}) async-start(), calls=%async_computation.8 | async-start | bytes 1179648 | tf_op jit(solution)/shard_map/all_gather | solution.py:125
  9.0 369.1 %all-gather.15.cloned.1.call-start = ((), (), s32[]{:S(2)}) async-start(), calls=%async_computation.20 | async-start | bytes 41943040 | tf_op jit(solution)/shard_map/all_gather | solution.py:19
  9.0 60.8 %copy-start.1 = (bf16[4096,1024]{1,0:T(8,128)(2,1)S(1)}, bf16[4096,1024]{1,0:T(8,128)(2,1)}, u32[]{:S(2)}) copy-start(bf16[4096,1024]{1,0:T(8,128)(2,1)} %param.30) | copy-start | bytes 25165828
  32.2 40.0 %copy-start.34 = (f32[1,1024]{1,0:T(1,128)}, f32[1,1024]{1,0:T(1,128)S(1)}, u32[]{:S(2)}) copy-start(f32[1,1024]{1,0:T(1,128)S(1)} %get-tuple-element.441) | copy-start | bytes 12292
  37.9 32.0 %copy-start.28 = (f32[4096]{0:T(1024)}, f32[4096]{0:T(1024)S(1)}, u32[]{:S(2)}) copy-start(f32[4096]{0:T(1024)S(1)} %get-tuple-element.438) | copy-start | bytes 49156
  69.9 2.3 copy-start.19
  72.1 3.2 copy-start.2
  164.8 6.5 copy-start.30
  164.8 13.4 copy-start.6
  164.8 13.4 copy-start.12
  164.8 13.4 copy-start.13
  164.8 7.8 copy-start.14
  171.3 1.3 copy-start.7
  178.2 2.0 copy-start.20
  178.2 1.2 copy-start.16
  178.3 261.7 %all-gather.9.cloned.1.call-start = ((), (), s32[]{:S(2)}) async-start(), calls=%async_computation.9 | async-start | bytes 3170304 | tf_op jit(solution)/shard_map/all_gather | solution.py:128
  180.2 303.6 %all-gather.11.cloned.1.call-start = ((), (), s32[]{:S(2)}) async-start(), calls=%async_computation.10 | async-start | bytes 1585152 | tf_op jit(solution)/shard_map/all_gather | solution.py:129
  181.0 502.3 %all-reduce.2.cloned.1.call-start = ((), (), s32[]{:S(2)}) async-start(), calls=%async_computation.12 | async-start | bytes 16777216 | tf_op jit(solution)/shard_map/psum | solution.py:179
  439.9 12.5 copy-start.10
  439.9 12.5 copy-start.40
  506.1 13.0 copy-start.42
  531.7 416.3 %all-gather.13.cloned.1.call-start = ((), (), s32[]{:S(2)}) async-start(), calls=%async_computation.18 | async-start | bytes 1310720 | tf_op jit(solution)/shard_map/all_gather | solution.py:214
  695.2 23.2 %copy-start.15 = (bf16[256,1024]{1,0:T(8,128)(2,1)S(1)}, bf16[256,1024]{1,0:T(8,128)(2,1)}, u32[]{:S(2)}) copy-start(bf16[256,1024]{1,0:T(8,128)(2,1)} %all_gather.30) | copy-start | bytes 1572868
  712.7 5.7 copy-start.5
  732.5 6.5 copy-start.4
  739.1 5.7 copy-start
  767.7 6.5 copy-start.4
  774.2 5.7 copy-start
  802.9 6.5 copy-start.4
  809.4 5.7 copy-start
  838.0 6.5 copy-start.4
  844.6 5.7 copy-start
  870.1 6.3 copy-start.3
  874.3 25.6 %copy-start.9 = (bf16[32,8,4,1024]{3,1,2,0:T(8,128)(2,1)}, bf16[32,8,4,1024]{3,1,2,0:T(8,128)(2,1)S(1)}, u32[]{:S(2)}) copy-start(bf16[32,8,4,1024]{3,1,2,0:T(8,128)(2,1)S(1)} %copy.128) | copy-start | bytes 6291460
  876.4 1.6 copy-start.27
  878.6 1.6 copy-start.11
  881.0 120.0 %reduce-scatter.25.cloned.1.call-start = ((), (), s32[]{:S(2)}) async-start(), calls=%async_computation.21 | async-start | bytes 589824
  881.0 18.9 %slice-start = ((s8[8388608]{0:T(1024)(128)(4,1)}), s8[4194304]{0:T(1024)(128)(4,1)S(1)}, s32[]{:S(2)}) async-start(s8[8388608]{0:T(1024)(128)(4,1)} %bitcast.205), calls=%async_computation.22 | async-start | bytes 8388608
  890.7 9.3 slice-start.1
  890.7 9.3 copy-start.29
  890.7 9.3 copy-start.35
  900.0 18.5 %copy-start.37 = (f32[1024]{0:T(1024)S(1)}, f32[1024]{0:T(1024)}, u32[]{:S(2)}) copy-start(f32[1024]{0:T(1024)} %get-tuple-element.368) | copy-start | bytes 12292
  919.5 139.1 %reduce-scatter.21.cloned.1.call-start = ((), (), s32[]{:S(2)}) async-start(), calls=%async_computation.17 | async-start | bytes 3170304 | tf_op jit(solution)/shard_map/reduce_scatter | solution.py:222
  919.6 11.7 copy-start.8
  931.3 193.6 %reduce-scatter.17.cloned.1.call-start = ((), (), s32[]{:S(2)}) async-start(), calls=%async_computation.15 | async-start | bytes 1179648 | tf_op jit(solution)/shard_map/reduce_scatter | solution.py:220
  940.5 250.0 %reduce-scatter.15.cloned.1.call-start = ((), (), s32[]{:S(2)}) async-start(), calls=%async_computation.14 | async-start | bytes 1179648 | tf_op jit(solution)/shard_map/reduce_scatter | solution.py:219
  948.0 314.2 %reduce-scatter.23.cloned.1.call-start = ((), (), s32[]{:S(2)}) async-start(), calls=%async_computation.19 | async-start | bytes 2359296 | tf_op jit(solution)/shard_map/reduce_scatter | solution.py:218
  950.9 422.9 %reduce-scatter.19.cloned.1.call-start = ((), (), s32[]{:S(2)}) async-start(), calls=%async_computation.16 | async-start | bytes 6340608 | tf_op jit(solution)/shard_map/reduce_scatter | solution.py:221
  971.3 3.1 copy-start.41
  974.4 474.4 %reduce-scatter.11.cloned.1.call-start = ((), (), s32[]{:S(2)}) async-start(), calls=%async_computation.11 | async-start | bytes 10485760 | tf_op jit(solution)/shard_map/reduce_scatter | solution.py:169
  986.2 536.7 %reduce-scatter.13.cloned.1.call-start = ((), (), s32[]{:S(2)}) async-start(), calls=%async_computation.13 | async-start | bytes 10485760 | tf_op jit(solution)/shard_map/reduce_scatter | solution.py:211
  999.4 0.9 copy-start.23
  999.4 1.1 copy-start.31
  999.4 1.2 copy-start.32
  999.4 1.4 copy-start.33
  999.5 428.6 %copy-start.25 = (f32[128,256]{1,0:T(8,128)S(1)}, f32[128,256]{1,0:T(8,128)}, u32[]{:S(2)}) copy-start(f32[128,256]{1,0:T(8,128)} %param.36) | copy-start | bytes 393220
  999.5 432.6 %copy-start.21 = (f32[688,128]{1,0:T(8,128)S(1)}, f32[688,128]{1,0:T(8,128)}, u32[]{:S(2)}) copy-start(f32[688,128]{1,0:T(8,128)} %param.48) | copy-start | bytes 1056772
  999.5 435.0 %copy-start.17 = (f32[2,128,688]{1,2,0:T(8,128)S(1)}, f32[2,128,688]{1,2,0:T(8,128)}, u32[]{:S(2)}) copy-start(f32[2,128,688]{1,2,0:T(8,128)} %param.44) | copy-start | bytes 2113540
  1002.1 416.4 %copy-start.38 = (f32[1,128]{1,0:T(1,128)}, f32[1,128]{1,0:T(1,128)S(1)}, u32[]{:S(2)}) copy-start(f32[1,128]{1,0:T(1,128)S(1)} %copy.124) | copy-start | bytes 1540
  1008.2 410.2 %copy-start.39 = (f32[1,128]{1,0:T(1,128)}, f32[1,128]{1,0:T(1,128)S(1)}, u32[]{:S(2)}) copy-start(f32[1,128]{1,0:T(1,128)S(1)} %psum.22) | copy-start | bytes 1540
  1058.6 373.4 %copy-start.22 = (f32[688,128]{1,0:T(8,128)S(1)}, f32[688,128]{1,0:T(8,128)}, u32[]{:S(2)}) copy-start(f32[688,128]{1,0:T(8,128)} %reduce-scatter.21.cloned.1.call-done) | copy-start | bytes 1056772
  1373.7 60.8 %copy-start.18 = (f32[2,128,688]{1,2,0:T(8,128)S(1)}, f32[2,128,688]{1,2,0:T(8,128)}, u32[]{:S(2)}) copy-start(f32[2,128,688]{1,2,0:T(8,128)} %reduce-scatter.19.cloned.1.call-done) | copy-start | bytes 2113540
  (1 other events, 0.7 us)
Sparse Core Ops, SparseCore 0:
  10.8 46.0 all-gather.6
  178.4 199.6 all-gather.14
  380.7 59.2 all-gather.8
  442.4 41.3 all-gather.10
  531.9 151.3 all-reduce.1
  881.1 16.8 all-gather.12
  919.7 62.0 reduce-scatter.24
  986.3 72.3 reduce-scatter.20
  1062.4 62.4 reduce-scatter.16
  1128.2 62.2 reduce-scatter.14
  1195.0 67.1 reduce-scatter.22
  1266.1 107.5 reduce-scatter.18
  1376.5 72.2 reduce-scatter.10
  1451.2 71.7 reduce-scatter.12
